TPU v7x, 32 devices: a whole 2x2x4 slice. The times are simulated.
32 devices in a mesh: area: 8 (over y, x, core), layer: 4 (over z).
Axes of the slice: x: 2, y: 2, z: 4, core: 2. Of those that a mesh axis runs over, the one named last changes fastest.
Arguments:
- permeability: float32 [16, 4096, 512], P('layer', 'area'), may hold values from 0.1 to 10
- mobility: float32 [16, 4096, 512], P('layer', 'area'), may hold values from 0.3 to 3
- thickness: float32 [16], P('layer'), may hold values from 0.5 to 2
- caprock: int32 [4096, 512], P('area'), may hold values from 0 to 7
- plume: int32 [4096, 512], P('area'), may hold values from 0 to 15
- storage: float32 [4096, 512], P('area'), may hold values from 1.6 to 16
- source: float32 [4096, 512], P('area'), may hold values from -192 to 192
- pressure_old: float32 [4096, 512], P('area'), may hold values from -6 to 6
Outputs:
- cell_pressure: float32 [16, 4096, 512], P('layer', 'area')
- flux_rows: float32 [16, 4096, 512], P('layer', 'area')
- flux_cols: float32 [16, 4096, 512], P('layer', 'area')
Inputs may be any that keep to these rules, and one draw needn't show every extreme that they name: Layers above layer caprock of a column are sealed rock. CO2 fills the open layers above layer plume of a column; where plume <= caprock a column holds no CO2.
All inputs are finite; a program needn't handle non-finite values.
Results may differ from a plain program's by a relative error of at most 0.0003.
Values sent between devices are 32-bit elements; how exact they have to be, the bound alone decides.
No kernel may reach another device: no remote copies, remote signals or barrier semaphores. Data moves between devices by JAX's collectives and lax.ppermute only.
A program may use at most 128 MiB of HBM per device.

v0:
```python
import jax
import jax.numpy as jnp
from jax import lax
from jax.sharding import PartitionSpec as P

SWEEPS = 3
buoyancy_scale = 0.3
gravity_scale = 0.05
gas_density = 0.7
brine_density = 1.0


def padded_2(block, sides, width):
    for axis, dim in sides:
        count = lax.axis_size(axis)
        forward = [(i, i + 1) for i in range(count - 1)]
        backward = [(target, source) for source, target in forward]
        low = lax.ppermute(
            lax.slice_in_dim(block, block.shape[dim] - width, None, axis=dim), axis, forward
        )
        high = lax.ppermute(lax.slice_in_dim(block, 0, width, axis=dim), axis, backward)
        block = jnp.concatenate([low, block, high], axis=dim)
    return block


def from_behind(block, axis, distance):
    devices = range(lax.axis_size(axis))
    route = [(i - distance, i) for i in devices if i - distance in devices]
    return lax.ppermute(block, axis, route)


def harmonic(near_value, far_value):
    summed = near_value + far_value
    divisor = jnp.where(summed > 0, summed, 1.0)
    return 2.0 * near_value * far_value / divisor


def neighbours(padded, row_count):
    widened = jnp.pad(padded, ((0, 0), (1, 1)))
    return [
        widened[0:row_count, 1:-1],
        widened[2 : row_count + 2, 1:-1],
        widened[1 : row_count + 1, 0:-2],
        widened[1 : row_count + 1, 2:],
    ]


def prepare(summed_pad, storage, source, pressure_old):
    row_count = storage.shape[0]
    trans_pad = summed_pad[0]
    buoy_pad = summed_pad[1]
    drive_pad = buoyancy_scale * summed_pad[2]
    trans_faces = [
        harmonic(trans_pad[1 : row_count + 1], neighbour)
        for neighbour in neighbours(trans_pad, row_count)
    ]
    buoy_faces = [
        harmonic(buoy_pad[1 : row_count + 1], neighbour)
        for neighbour in neighbours(buoy_pad, row_count)
    ]
    drive_centre = drive_pad[1 : row_count + 1]
    gravity_drive = sum(
        (
            face_coef * (neighbour - drive_centre)
            for face_coef, neighbour in zip(buoy_faces, neighbours(drive_pad, row_count))
        )
    )
    right_hand = storage * pressure_old + source + gravity_drive
    diagonal = storage + trans_faces[0] + trans_faces[1] + trans_faces[2] + trans_faces[3]
    return (trans_faces, right_hand, diagonal)


def relax(trans_faces, right_hand, diagonal, padded):
    row_count = right_hand.shape[0]
    inflow = sum(
        (
            face_coef * neighbour
            for face_coef, neighbour in zip(trans_faces, neighbours(padded, row_count))
        )
    )
    return (right_hand + inflow) / diagonal


def column_depths(every_thick, layer_count, caprock, plume, limit):
    block_count = every_thick.shape[0] // layer_count

    def add_block(block, carry):
        height, above = carry
        first = block * layer_count
        thick_block = lax.dynamic_slice_in_dim(every_thick, first, layer_count, 0)[:, None, None]
        depth = first + lax.broadcasted_iota(jnp.int32, (layer_count, 1, 1), 0)
        gas = (depth >= caprock[None]) & (depth < plume[None])
        height = height + jnp.sum(jnp.where(gas, thick_block, 0.0), axis=0)
        above = above + jnp.sum(jnp.where(gas & (depth < limit), thick_block, 0.0), axis=0)
        return (height, above)

    zeros = jnp.zeros(caprock.shape, jnp.float32)
    return lax.fori_loop(0, block_count, add_block, (zeros, zeros))


def local(permeability, mobility, thickness, caprock, plume, storage, source, pressure_old):
    layer_count = permeability.shape[0]
    layer_index = lax.axis_index("layer")
    layers = layer_index * layer_count + lax.broadcasted_iota(jnp.int32, permeability.shape, 0)
    open_cell = layers >= caprock[None]
    gas_cell = open_cell & (layers < plume[None])
    layer_thick = thickness[:, None, None]
    conduct = jnp.where(open_cell, permeability * mobility * layer_thick, 0.0)
    every_thick = lax.all_gather(thickness, "layer", axis=0, tiled=True)
    limit = layer_index * layer_count
    gas_height, gas_above = column_depths(every_thick, layer_count, caprock, plume, limit)
    column_parts = jnp.stack(
        [jnp.sum(conduct, axis=0), jnp.sum(jnp.where(gas_cell, conduct, 0.0), axis=0)]
    )
    summed = lax.psum(column_parts, "layer")
    summed = jnp.concatenate([summed, gas_height[None]], axis=0)
    padded = padded_2(summed, (("area", 1),), 1)
    trans_faces, right_hand, diagonal = prepare(padded, storage, source, pressure_old)
    pressure = pressure_old
    for sweep_index in range(SWEEPS):
        pressure_pad = padded_2(pressure, (("area", 0),), 1)
        pressure = relax(trans_faces, right_hand, diagonal, pressure_pad)
    layer_mass = layer_thick * jnp.where(gas_cell, gas_density, brine_density)
    depth_all = lax.broadcasted_iota(jnp.int32, every_thick.shape, 0)
    thick_over = jnp.sum(jnp.where(depth_all < limit, every_thick, 0.0))
    mass_over = thick_over - (brine_density - gas_density) * gas_above
    hydro_head = mass_over[None] + jnp.cumsum(layer_mass, axis=0) - 0.5 * layer_mass
    cell_pressure = pressure[None] + gravity_scale * hydro_head
    edge_rows = jnp.stack([conduct[:, 0, :], cell_pressure[:, 0, :]])
    beyond = from_behind(edge_rows, "area", -1)
    next_conduct = jnp.concatenate([conduct[:, 1:, :], beyond[0][:, None, :]], axis=1)
    next_pressure = jnp.concatenate([cell_pressure[:, 1:, :], beyond[1][:, None, :]], axis=1)
    flux_rows = harmonic(conduct, next_conduct) * (cell_pressure - next_pressure)
    side_conduct = jnp.pad(conduct[:, :, 1:], ((0, 0), (0, 0), (0, 1)))
    side_pressure = jnp.pad(cell_pressure[:, :, 1:], ((0, 0), (0, 0), (0, 1)))
    flux_cols = harmonic(conduct, side_conduct) * (cell_pressure - side_pressure)
    return (cell_pressure, flux_rows, flux_cols)


def solution(mesh):
    in_specs = (
        P("layer", "area", None),
        P("layer", "area", None),
        P("layer"),
        P("area", None),
        P("area", None),
        P("area", None),
        P("area", None),
        P("area", None),
    )
    out_specs = (P("layer", "area", None), P("layer", "area", None), P("layer", "area", None))
    return jax.shard_map(local, mesh=mesh, in_specs=in_specs, out_specs=out_specs, check_vma=False)
```

profile of v0, /device:TPU:4, one launch (start us, length us, event | category | flops | bytes accessed | tf_op | source)
XLA Modules:
  0.0 176.6 jit_solution(2895812345910085846)
XLA Ops:
  8.0 1.9 %collective-permute-start.2 = (f32[1,512]{1,0:T(1,128)S(1)}, f32[1,512]{1,0:T(1,128)S(1)}, u32[]{:S(2)}, u32[]{:S(2)}) collective-permute-start(f32[1,512]{1,0:T(1,128)S(1)} %get-tuple-element.191), channel_id=1, source_target_pairs={{0,4},{4,8},{8,12},{12,16},{16,20},{20,24},{24,28},{1,5},{5,9},{9,... | collective-permute-start | bytes 6152 | tf_op jit(solution)/shard_map/ppermute | solution.py:18
  9.9 4.5 %collective-permute-start.3 = (f32[1,512]{1,0:T(1,128)S(1)}, f32[1,512]{1,0:T(1,128)S(1)}, u32[]{:S(2)}, u32[]{:S(2)}) collective-permute-start(f32[1,512]{1,0:T(1,128)S(1)} %get-tuple-element.192), channel_id=1, source_target_pairs={{4,0},{8,4},{12,8},{16,12},{20,16},{24,20},{28,24},{5,1},{9,5},{13... | collective-permute-start | bytes 6152 | tf_op jit(solution)/shard_map/ppermute | solution.py:21
  14.4 7.8 %fusion.59 = (f32[512,512]{1,0:T(8,128)S(1)}, f32[512,512]{1,0:T(8,128)S(1)}, f32[4,512,512]{2,1,0:T(8,128)}) fusion(s32[512,512]{1,0:T(8,128)} %param.14, s32[512,512]{1,0:T(8,128)} %param.13, s32[4]{0:T(128)S(1)} %iota_add_fusion.1, f32[4]{0:T(128)} %param.12, f32[4,512,512]{2,1,0:T(8,128)} %param.10, f32[4,512,512]{2,1,0:T(8,128)} %param.11), kind=kLoop, calls=%fused_computation.138 | loop fusion | flops 8912896 | bytes 16777248 | tf_op jit(solution)/shard_map/reduce_sum | solution.py:113
  22.2 1.5 pad_maximum_fusion.2
  25.2 12.4 %all-reduce.8 = f32[16]{0:T(128)S(1)} all-reduce(f32[16]{0:T(128)S(1)} %dynamic-update-slice), channel_id=1, replica_groups=mesh['area'=8,'layer'=4] {'layer'}, use_global_device_ids=true, to_apply=%add.8 | all-reduce | flops 16 | bytes 128
  37.6 12.6 %while.16 = (s32[]{:T(128)}, f32[512,512]{1,0:T(8,128)S(1)}, f32[512,512]{1,0:T(8,128)}, s32[512,512]{1,0:T(8,128)S(1)}, s32[512,512]{1,0:T(8,128)S(1)}, /*index...) while((s32[]{:T(128)}, f32[512,512]{1,0:T(8,128)S(1)}, ...), condition=%wide.region_6.7_spmd.clone, body=%wide.region_3.0_spmd.clone.sunk | while | flops 8912915 | bytes 18874700 | solution.py:98
  37.7 1.3 select_reduce_fusion.4
  39.8 1.0 copy-done.6
  40.8 1.3 select_reduce_fusion.4
  42.9 1.0 copy-done.6
  44.0 1.3 select_reduce_fusion.4
  46.1 1.0 copy-done.6
  47.1 1.3 select_reduce_fusion.4
  49.2 1.0 copy-done.6
  50.8 59.5 %all-reduce.11.cloned.1.call-done = f32[2,512,512]{2,1,0:T(8,128)} async-done(((f32[2,512,512]{2,1,0:T(8,128)}), f32[2,512,512]{2,1,0:T(8,128)}) %all-reduce.11.cloned.1.call-update) | async-done | bytes 2097168 | tf_op jit(solution)/shard_map/psum | solution.py:115
  111.3 1.9 %collective-permute-start = (f32[3,1,512]{2,1,0:T(1,128)S(1)}, f32[3,1,512]{2,1,0:T(1,128)S(1)}, u32[]{:S(2)}, u32[]{:S(2)}) collective-permute-start(f32[3,1,512]{2,1,0:T(1,128)S(1)} %get-tuple-element.185), channel_id=1, source_target_pairs={{0,4},{4,8},{8,12},{12,16},{16,20},{20,24},{24,28},{1,5},{5,9},{9,... | collective-permute-start | bytes 18440 | tf_op jit(solution)/shard_map/ppermute | solution.py:18
  113.2 4.5 %collective-permute-start.1 = (f32[3,1,512]{2,1,0:T(1,128)S(1)}, f32[3,1,512]{2,1,0:T(1,128)S(1)}, u32[]{:S(2)}, u32[]{:S(2)}) collective-permute-start(f32[3,1,512]{2,1,0:T(1,128)S(1)} %get-tuple-element.186), channel_id=1, source_target_pairs={{4,0},{8,4},{12,8},{16,12},{20,16},{24,20},{28,24},{5,1},{9,5},{13... | collective-permute-start | bytes 18440 | tf_op jit(solution)/shard_map/ppermute | solution.py:21
  117.8 1.6 select_maximum_fusion.4
  121.8 6.4 %fusion.46 = (f32[512,512]{1,0:T(8,128)S(1)}, f32[512,512]{1,0:T(8,128)S(1)}, f32[512,512]{1,0:T(8,128)S(1)}, f32[512,512]{1,0:T(8,128)S(1)}) fusion(f32[514,514]{1,0:T(8,128)S(1)} %select_maximum_fusion.4, f32[1,512]{1,0:T(1,128)S(1)} %collective-permute-done.3, f32[512,512]{1,0:T(8,128)S(1)} %copy-done.9, f32[1,512]{1,0:T(1,128)S(1)} %collective-permute-done.2, ...), kind=kLoop, calls=%fused_computation.98 | loop fusion | flops 20709376 | bytes 21037056 | tf_op jit(solution)/shard_map/div | solution.py:81
  128.2 2.2 %collective-permute-start.4 = (f32[1,512]{1,0:T(1,128)S(1)}, f32[1,512]{1,0:T(1,128)S(1)}, u32[]{:S(2)}, u32[]{:S(2)}) collective-permute-start(f32[1,512]{1,0:T(1,128)S(1)} %get-tuple-element.189), channel_id=1, source_target_pairs={{0,4},{4,8},{8,12},{12,16},{16,20},{20,24},{24,28},{1,5},{5,9},{9,... | collective-permute-start | bytes 6152 | tf_op jit(solution)/shard_map/ppermute | solution.py:18
  130.4 4.3 %collective-permute-start.5 = (f32[1,512]{1,0:T(1,128)S(1)}, f32[1,512]{1,0:T(1,128)S(1)}, u32[]{:S(2)}, u32[]{:S(2)}) collective-permute-start(f32[1,512]{1,0:T(1,128)S(1)} %get-tuple-element.190), channel_id=1, source_target_pairs={{4,0},{8,4},{12,8},{16,12},{20,16},{24,20},{28,24},{5,1},{9,5},{13... | collective-permute-start | bytes 6152 | tf_op jit(solution)/shard_map/ppermute | solution.py:21
  136.4 1.7 fusion.39
  138.2 1.9 %collective-permute-start.6 = (f32[1,512]{1,0:T(1,128)S(1)}, f32[1,512]{1,0:T(1,128)S(1)}, u32[]{:S(2)}, u32[]{:S(2)}) collective-permute-start(f32[1,512]{1,0:T(1,128)S(1)} %get-tuple-element.187), channel_id=1, source_target_pairs={{0,4},{4,8},{8,12},{12,16},{16,20},{20,24},{24,28},{1,5},{5,9},{9,... | collective-permute-start | bytes 6152 | tf_op jit(solution)/shard_map/ppermute | solution.py:18
  140.1 4.7 %collective-permute-start.7 = (f32[1,512]{1,0:T(1,128)S(1)}, f32[1,512]{1,0:T(1,128)S(1)}, u32[]{:S(2)}, u32[]{:S(2)}) collective-permute-start(f32[1,512]{1,0:T(1,128)S(1)} %get-tuple-element.188), channel_id=1, source_target_pairs={{4,0},{8,4},{12,8},{16,12},{20,16},{24,20},{28,24},{5,1},{9,5},{13... | collective-permute-start | bytes 6152 | tf_op jit(solution)/shard_map/ppermute | solution.py:21
  144.8 1.1 collective-permute-done.7
  146.4 1.7 fusion.32
  148.1 2.2 %multiply_add_fusion = f32[4,512,512]{2,1,0:T(8,128)S(1)} fusion(f32[512,512]{1,0:T(8,128)S(1)} %multiply_subtract_fusion, f32[512,512]{1,0:T(8,128)S(1)} %fusion.32, s32[512,512]{1,0:T(8,128)S(1)} %get-tuple-element.281, f32[4]{0:T(128)S(1)} %copy-done.11, s32[512,512]{1,0:T(8,128)S(1)} %get-tuple-element.280, s32[4]{0:T(128)S(1)} %iota_add_fusion.1), kind=kOutput, calls=%fused_computation.17 | output fusion | flops 18874368 | bytes 8388640 | tf_op jit(solution)/shard_map/jit(cumsum)/reduce_window_sum | solution.py:127
  150.3 4.5 %collective-permute-start.8 = (f32[2,4,512]{2,0,1:T(2,128)S(1)}, f32[2,4,512]{2,0,1:T(2,128)S(1)}, u32[]{:S(2)}, u32[]{:S(2)}) collective-permute-start(f32[2,4,512]{2,0,1:T(2,128)S(1)} %pad_maximum_fusion.13), channel_id=1, source_target_pairs={{4,0},{8,4},{12,8},{16,12},{20,16},{24,20},{28,24},{5,1},{9,5},{13... | collective-permute-start | bytes 49160 | tf_op jit(solution)/shard_map/ppermute | solution.py:29
  155.5 1.1 slice.282
  156.6 3.1 %slice.283 = f32[4,512,511]{2,1,0:T(8,128)} slice(f32[4,512,512]{2,1,0:T(8,128)S(1)} %multiply_add_fusion), slice={[0:4], [0:512], [1:512]} | slice | bytes 8372224 | tf_op jit(solution)/shard_map/slice | solution.py:135
  159.7 2.5 %slice.280 = f32[4,511,512]{2,1,0:T(8,128)} slice(f32[4,512,512]{2,1,0:T(8,128)S(1)} %multiply_add_fusion), slice={[0:4], [1:512], [0:512]} | slice | bytes 8372224 | tf_op jit(solution)/shard_map/slice | solution.py:132
  162.3 7.4 %fusion.3 = (f32[4,512,512]{2,1,0:T(8,128)}, f32[4,512,512]{2,1,0:T(8,128)}) fusion(f32[4,512,512]{2,1,0:T(8,128)S(1)} %multiply_add_fusion, f32[4,512,511]{2,1,0:T(8,128)} %slice.283, f32[4,512,512]{2,1,0:T(8,128)S(1)} %copy-done.1, f32[4,512,511]{2,1,0:T(8,128)S(1)} %slice.282, f32[4,1,512]{2,1,0:T(1,128)S(1)} %get-tuple-element.194, ...), kind=kLoop, calls=%fused_computation.14 | loop fusion | flops 17825792 | bytes 33538048 | tf_op jit(solution)/shard_map/mul | solution.py:136
  (81 shorter events, 11.6 us)
Async XLA Ops:
  7.2 103.2 %all-reduce.11.cloned.1.call-start = ((), (), s32[]{:S(2)}) async-start(), calls=%async_computation | async-start | bytes 4194304 | tf_op jit(solution)/shard_map/psum | solution.py:115
  8.0 109.8 %collective-permute-start.2 = (f32[1,512]{1,0:T(1,128)S(1)}, f32[1,512]{1,0:T(1,128)S(1)}, u32[]{:S(2)}, u32[]{:S(2)}) collective-permute-start(f32[1,512]{1,0:T(1,128)S(1)} %get-tuple-element.191), channel_id=1, source_target_pairs={{0,4},{4,8},{8,12},{12,16},{16,20},{20,24},{24,28},{1,5},{5,9},{9,... | collective-permute-start | bytes 6152 | tf_op jit(solution)/shard_map/ppermute | solution.py:18
  9.9 107.9 %collective-permute-start.3 = (f32[1,512]{1,0:T(1,128)S(1)}, f32[1,512]{1,0:T(1,128)S(1)}, u32[]{:S(2)}, u32[]{:S(2)}) collective-permute-start(f32[1,512]{1,0:T(1,128)S(1)} %get-tuple-element.192), channel_id=1, source_target_pairs={{4,0},{8,4},{12,8},{16,12},{20,16},{24,20},{28,24},{5,1},{9,5},{13... | collective-permute-start | bytes 6152 | tf_op jit(solution)/shard_map/ppermute | solution.py:21
  22.2 1.6 copy-start.12
  22.2 2.7 %copy-start.11 = (f32[4]{0:T(128)S(1)}, f32[4]{0:T(128)}, u32[]{:S(2)}) copy-start(f32[4]{0:T(128)} %param.12) | copy-start | bytes 52
  22.2 15.4 %copy-start.2 = (s32[512,512]{1,0:T(8,128)S(1)}, s32[512,512]{1,0:T(8,128)}, u32[]{:S(2)}) copy-start(s32[512,512]{1,0:T(8,128)} %param.13) | copy-start | bytes 3145732
  22.2 15.4 %copy-start.3 = (s32[512,512]{1,0:T(8,128)S(1)}, s32[512,512]{1,0:T(8,128)}, u32[]{:S(2)}) copy-start(s32[512,512]{1,0:T(8,128)} %param.14) | copy-start | bytes 3145732
  37.6 1.4 copy-start.5
  39.8 1.0 copy-start.6
  40.8 1.4 copy-start.5
  42.9 1.0 copy-start.6
  43.9 1.4 copy-start.5
  46.1 1.0 copy-start.6
  47.0 1.4 copy-start.5
  49.2 1.0 copy-start.6
  110.3 9.1 %copy-start.4 = (f32[2,512,512]{2,1,0:T(8,128)S(1)}, f32[2,512,512]{2,1,0:T(8,128)}, u32[]{:S(2)}) copy-start(f32[2,512,512]{2,1,0:T(8,128)} %all-reduce.11.cloned.1.call-done) | copy-start | bytes 6291460
  111.3 8.2 %collective-permute-start = (f32[3,1,512]{2,1,0:T(1,128)S(1)}, f32[3,1,512]{2,1,0:T(1,128)S(1)}, u32[]{:S(2)}, u32[]{:S(2)}) collective-permute-start(f32[3,1,512]{2,1,0:T(1,128)S(1)} %get-tuple-element.185), channel_id=1, source_target_pairs={{0,4},{4,8},{8,12},{12,16},{16,20},{20,24},{24,28},{1,5},{5,9},{9,... | collective-permute-start | bytes 18440 | tf_op jit(solution)/shard_map/ppermute | solution.py:18
  113.2 6.2 %collective-permute-start.1 = (f32[3,1,512]{2,1,0:T(1,128)S(1)}, f32[3,1,512]{2,1,0:T(1,128)S(1)}, u32[]{:S(2)}, u32[]{:S(2)}) collective-permute-start(f32[3,1,512]{2,1,0:T(1,128)S(1)} %get-tuple-element.186), channel_id=1, source_target_pairs={{4,0},{8,4},{12,8},{16,12},{20,16},{24,20},{28,24},{5,1},{9,5},{13... | collective-permute-start | bytes 18440 | tf_op jit(solution)/shard_map/ppermute | solution.py:21
  119.9 1.2 copy-start.8
  119.9 1.5 copy-start.9
  119.9 1.8 %copy-start.10 = (f32[512,512]{1,0:T(8,128)S(1)}, f32[512,512]{1,0:T(8,128)}, u32[]{:S(2)}) copy-start(f32[512,512]{1,0:T(8,128)} %param.16) | copy-start | bytes 3145732
  121.8 12.9 %copy-start.7 = (f32[512,512]{1,0:T(8,128)S(1)}, f32[512,512]{1,0:T(8,128)}, u32[]{:S(2)}) copy-start(f32[512,512]{1,0:T(8,128)} %get-tuple-element.129) | copy-start | bytes 3145732
  128.2 7.2 %collective-permute-start.4 = (f32[1,512]{1,0:T(1,128)S(1)}, f32[1,512]{1,0:T(1,128)S(1)}, u32[]{:S(2)}, u32[]{:S(2)}) collective-permute-start(f32[1,512]{1,0:T(1,128)S(1)} %get-tuple-element.189), channel_id=1, source_target_pairs={{0,4},{4,8},{8,12},{12,16},{16,20},{20,24},{24,28},{1,5},{5,9},{9,... | collective-permute-start | bytes 6152 | tf_op jit(solution)/shard_map/ppermute | solution.py:18
  130.4 5.6 %collective-permute-start.5 = (f32[1,512]{1,0:T(1,128)S(1)}, f32[1,512]{1,0:T(1,128)S(1)}, u32[]{:S(2)}, u32[]{:S(2)}) collective-permute-start(f32[1,512]{1,0:T(1,128)S(1)} %get-tuple-element.190), channel_id=1, source_target_pairs={{4,0},{8,4},{12,8},{16,12},{20,16},{24,20},{28,24},{5,1},{9,5},{13... | collective-permute-start | bytes 6152 | tf_op jit(solution)/shard_map/ppermute | solution.py:21
  136.4 8.4 %copy-start.1 = (f32[4,512,512]{2,1,0:T(8,128)S(1)}, f32[4,512,512]{2,1,0:T(8,128)}, u32[]{:S(2)}) copy-start(f32[4,512,512]{2,1,0:T(8,128)} %get-tuple-element.176) | copy-start | bytes 12582916
  138.2 6.7 %collective-permute-start.6 = (f32[1,512]{1,0:T(1,128)S(1)}, f32[1,512]{1,0:T(1,128)S(1)}, u32[]{:S(2)}, u32[]{:S(2)}) collective-permute-start(f32[1,512]{1,0:T(1,128)S(1)} %get-tuple-element.187), channel_id=1, source_target_pairs={{0,4},{4,8},{8,12},{12,16},{16,20},{20,24},{24,28},{1,5},{5,9},{9,... | collective-permute-start | bytes 6152 | tf_op jit(solution)/shard_map/ppermute | solution.py:18
  140.1 5.8 %collective-permute-start.7 = (f32[1,512]{1,0:T(1,128)S(1)}, f32[1,512]{1,0:T(1,128)S(1)}, u32[]{:S(2)}, u32[]{:S(2)}) collective-permute-start(f32[1,512]{1,0:T(1,128)S(1)} %get-tuple-element.188), channel_id=1, source_target_pairs={{4,0},{8,4},{12,8},{16,12},{20,16},{24,20},{28,24},{5,1},{9,5},{13... | collective-permute-start | bytes 6152 | tf_op jit(solution)/shard_map/ppermute | solution.py:21
  150.3 12.0 %copy-start = (f32[4,512,512]{2,1,0:T(8,128)}, f32[4,512,512]{2,1,0:T(8,128)S(1)}, u32[]{:S(2)}) copy-start(f32[4,512,512]{2,1,0:T(8,128)S(1)} %multiply_add_fusion) | copy-start | bytes 12582916
  150.3 11.9 %collective-permute-start.8 = (f32[2,4,512]{2,0,1:T(2,128)S(1)}, f32[2,4,512]{2,0,1:T(2,128)S(1)}, u32[]{:S(2)}, u32[]{:S(2)}) collective-permute-start(f32[2,4,512]{2,0,1:T(2,128)S(1)} %pad_maximum_fusion.13), channel_id=1, source_target_pairs={{4,0},{8,4},{12,8},{16,12},{20,16},{24,20},{28,24},{5,1},{9,5},{13... | collective-permute-start | bytes 49160 | tf_op jit(solution)/shard_map/ppermute | solution.py:29
Sparse Core Ops, SparseCore 0:
  23.9 86.4 all-reduce.10
where the time goes:
time: 177 us
  waiting for transfers between devices  61.2 us (35%)
  other arithmetic  42.7 us (24%)
  starting transfers between devices  30.6 us (17%)
  between operations  15 us (8%)
  local copies, waits for them, and re-layouts  14.7 us (8%)
  blocking collectives  12.4 us (7%)
    psum x1, waiting for transfers between devices, local(): summed = lax.psum(column_parts, 'layer')  59.5 us
    ppermute x4, starting transfers between devices, padded_2(): lax.ppermute(lax.slice_in_dim(block, 0, width, axis=dim), axis, backward)  18.1 us
    unnamed x1, blocking collectives  12.4 us
    div x3, other arithmetic, relax(): return (right_hand + inflow) / diagonal  9.84 us
    ppermute x4, starting transfers between devices, padded_2(): lax.ppermute(lax.slice_in_dim(block, block.shape[dim] - width, None, axis...  7.92 us
    reduce_sum x1, other arithmetic, local(): jnp.sum(conduct, axis=0)  7.77 us
    mul x1, other arithmetic, local(): harmonic(conduct, side_conduct) * (cell_pressure - side_pressure)  7.44 us
    reduce_sum x4, other arithmetic, add_block(): jnp.sum(jnp.where(gas & (depth < limit), thick_block, 0.0), axis=0)  5.35 us
  transfers between devices with their start and end apart: 10, of which 3 were waited for; matrix products, arithmetic and copies ran while one was open for 17% of the time, Pallas kernels for 0%

commit v1 on v0

--- a/solution.py
+++ b/solution.py
@@ -112,7 +112,7 @@
     column_parts = jnp.stack(
         [jnp.sum(conduct, axis=0), jnp.sum(jnp.where(gas_cell, conduct, 0.0), axis=0)]
     )
-    summed = lax.psum(column_parts, "layer")
+    summed = jnp.sum(lax.all_gather(column_parts, "layer"), axis=0)
     summed = jnp.concatenate([summed, gas_height[None]], axis=0)
     padded = padded_2(summed, (("area", 1),), 1)
     trans_faces, right_hand, diagonal = prepare(padded, storage, source, pressure_old)

time: 177 us -> 236 us (1.33)
  waiting for transfers between devices: 61.2 us -> 118 us
  other arithmetic: 42.7 us -> 45.9 us
    all_gather x0 -> x1, waiting for transfers between devices: none -> 117 us  [local(): summed = jnp.sum(lax.all_gather(column_parts, 'layer'), axis=0)]
    psum x1 -> x0, waiting for transfers between devices: 59.5 us -> none  [local(): summed = lax.psum(column_parts, 'layer')]
    reduce_sum x0 -> x1, other arithmetic: none -> 4.65 us  [local(): summed = jnp.sum(lax.all_gather(column_parts, 'layer'), axis=0)]
  transfers between devices with their start and end apart: 10 -> 10, of which waited for: 3 -> 3; matrix products, arithmetic and copies ran while one was open for 17% -> 10% of each run, Pallas kernels for 0% -> 0%
where the time goes in v1:
time: 236 us; the launch traced here: 235 us
  waiting for transfers between devices  118 us (50%)
  other arithmetic  45.9 us (19%)
  starting transfers between devices  30.6 us (13%)
  between operations  15.1 us (6%)
  local copies, waits for them, and re-layouts  12.7 us (5%)
  blocking collectives  12.5 us (5%)
    all_gather x1, waiting for transfers between devices, local(): summed = jnp.sum(lax.all_gather(column_parts, 'layer'), axis=0)  117 us
    ppermute x4, starting transfers between devices, padded_2(): lax.ppermute(lax.slice_in_dim(block, 0, width, axis=dim), axis, backward)  18.1 us
    unnamed x1, blocking collectives  12.5 us
    div x3, other arithmetic, relax(): return (right_hand + inflow) / diagonal  9.97 us
    ppermute x4, starting transfers between devices, padded_2(): lax.ppermute(lax.slice_in_dim(block, block.shape[dim] - width, None, axis...  7.89 us
    reduce_sum x1, other arithmetic, local(): jnp.sum(conduct, axis=0)  7.77 us
    mul x1, other arithmetic, local(): harmonic(conduct, side_conduct) * (cell_pressure - side_pressure)  6.8 us
    reduce_sum x4, other arithmetic, add_block(): jnp.sum(jnp.where(gas & (depth < limit), thick_block, 0.0), axis=0)  5.35 us
  transfers between devices with their start and end apart: 10, of which 3 were waited for; matrix products, arithmetic and copies ran while one was open for 10% of the time, Pallas kernels for 0%

profile of v1, /device:TPU:4, one launch (start us, length us, event | category | flops | bytes accessed | tf_op | source)
XLA Modules:
  0.0 235.1 jit_solution(4518132792143774374)
XLA Ops:
  7.2 7.8 %fusion.59 = (f32[512,512]{1,0:T(8,128)S(1)}, f32[512,512]{1,0:T(8,128)S(1)}, f32[4,512,512]{2,1,0:T(8,128)}) fusion(s32[512,512]{1,0:T(8,128)} %param.14, s32[512,512]{1,0:T(8,128)} %param.13, s32[4]{0:T(128)S(1)} %iota_add_fusion.1, f32[4]{0:T(128)} %param.12, f32[4,512,512]{2,1,0:T(8,128)} %param.10, f32[4,512,512]{2,1,0:T(8,128)} %param.11), kind=kLoop, calls=%fused_computation.138 | loop fusion | flops 8912896 | bytes 16777248 | tf_op jit(solution)/shard_map/reduce_sum | solution.py:113
  15.0 1.5 pad_maximum_fusion.2
  17.3 1.9 collective-permute-start.2
  19.2 4.5 %collective-permute-start.3 = (f32[1,512]{1,0:T(1,128)S(1)}, f32[1,512]{1,0:T(1,128)S(1)}, u32[]{:S(2)}, u32[]{:S(2)}) collective-permute-start(f32[1,512]{1,0:T(1,128)S(1)} %get-tuple-element.192), channel_id=1, source_target_pairs={{4,0},{8,4},{12,8},{16,12},{20,16},{24,20},{28,24},{5,1},{9,5},{13... | collective-permute-start | bytes 6152 | tf_op jit(solution)/shard_map/ppermute | solution.py:21
  25.3 12.5 %all-reduce.8 = f32[16]{0:T(128)S(1)} all-reduce(f32[16]{0:T(128)S(1)} %dynamic-update-slice), channel_id=1, replica_groups=mesh['area'=8,'layer'=4] {'layer'}, use_global_device_ids=true, to_apply=%add.8 | all-reduce | flops 16 | bytes 128
  38.4 12.6 %while.16 = (s32[]{:T(128)}, f32[512,512]{1,0:T(8,128)S(1)}, f32[512,512]{1,0:T(8,128)}, s32[512,512]{1,0:T(8,128)S(1)}, s32[512,512]{1,0:T(8,128)S(1)}, /*index...) while((s32[]{:T(128)}, f32[512,512]{1,0:T(8,128)S(1)}, ...), condition=%wide.region_6.7_spmd.clone, body=%wide.region_3.0_spmd.clone.sunk | while | flops 8912915 | bytes 18874700 | solution.py:98
  38.5 1.3 select_reduce_fusion.4
  40.6 1.0 copy-done.7
  41.6 1.3 select_reduce_fusion.4
  43.7 1.0 copy-done.7
  44.8 1.3 select_reduce_fusion.4
  46.9 1.0 copy-done.7
  47.9 1.3 select_reduce_fusion.4
  51.0 116.6 %all-gather.3.cloned.1.call-done = f32[8,512,512]{2,1,0:T(8,128)} async-done(((f32[2,512,512]{2,1,0:T(8,128)}), f32[8,512,512]{2,1,0:T(8,128)}) %all-gather.3.cloned.1.call-update) | async-done | bytes 8388624 | tf_op jit(solution)/shard_map/all_gather | solution.py:115
  167.6 4.7 %reduce_sum.64 = f32[2,512,512]{2,1,0:T(8,128)S(1)} reduce(f32[4,2,512,512]{3,2,1,0:T(8,128)} %bitcast.90, f32[]{:T(128)} %constant.56.clone.1), dimensions={0}, to_apply=%region_2.3 | reduce | flops 1572864 | bytes 10485764 | tf_op jit(solution)/shard_map/reduce_sum | solution.py:115
  172.3 1.9 collective-permute-start
  174.2 4.5 %collective-permute-start.1 = (f32[3,1,512]{2,1,0:T(1,128)S(1)}, f32[3,1,512]{2,1,0:T(1,128)S(1)}, u32[]{:S(2)}, u32[]{:S(2)}) collective-permute-start(f32[3,1,512]{2,1,0:T(1,128)S(1)} %get-tuple-element.186), channel_id=1, source_target_pairs={{4,0},{8,4},{12,8},{16,12},{20,16},{24,20},{28,24},{5,1},{9,5},{13... | collective-permute-start | bytes 18440 | tf_op jit(solution)/shard_map/ppermute | solution.py:21
  178.8 1.6 select_maximum_fusion.4
  182.8 6.5 %fusion.46 = (f32[512,512]{1,0:T(8,128)S(1)}, f32[512,512]{1,0:T(8,128)S(1)}, f32[512,512]{1,0:T(8,128)S(1)}, f32[512,512]{1,0:T(8,128)S(1)}) fusion(f32[514,514]{1,0:T(8,128)S(1)} %select_maximum_fusion.4, f32[1,512]{1,0:T(1,128)S(1)} %collective-permute-done.3, f32[512,512]{1,0:T(8,128)S(1)} %copy-done.10, f32[1,512]{1,0:T(1,128)S(1)} %collective-permute-done.2, ...), kind=kLoop, calls=%fused_computation.98 | loop fusion | flops 20709376 | bytes 21037056 | tf_op jit(solution)/shard_map/div | solution.py:81
  189.2 2.1 collective-permute-start.4
  191.4 4.3 %collective-permute-start.5 = (f32[1,512]{1,0:T(1,128)S(1)}, f32[1,512]{1,0:T(1,128)S(1)}, u32[]{:S(2)}, u32[]{:S(2)}) collective-permute-start(f32[1,512]{1,0:T(1,128)S(1)} %get-tuple-element.190), channel_id=1, source_target_pairs={{4,0},{8,4},{12,8},{16,12},{20,16},{24,20},{28,24},{5,1},{9,5},{13... | collective-permute-start | bytes 6152 | tf_op jit(solution)/shard_map/ppermute | solution.py:21
  197.5 1.8 fusion.39
  199.2 1.9 collective-permute-start.6
  201.2 4.7 %collective-permute-start.7 = (f32[1,512]{1,0:T(1,128)S(1)}, f32[1,512]{1,0:T(1,128)S(1)}, u32[]{:S(2)}, u32[]{:S(2)}) collective-permute-start(f32[1,512]{1,0:T(1,128)S(1)} %get-tuple-element.188), channel_id=1, source_target_pairs={{4,0},{8,4},{12,8},{16,12},{20,16},{24,20},{28,24},{5,1},{9,5},{13... | collective-permute-start | bytes 6152 | tf_op jit(solution)/shard_map/ppermute | solution.py:21
  205.9 1.1 collective-permute-done.7
  207.5 1.7 fusion.32
  209.2 2.2 multiply_add_fusion
  211.5 4.5 %collective-permute-start.8 = (f32[2,4,512]{2,0,1:T(2,128)S(1)}, f32[2,4,512]{2,0,1:T(2,128)S(1)}, u32[]{:S(2)}, u32[]{:S(2)}) collective-permute-start(f32[2,4,512]{2,0,1:T(2,128)S(1)} %pad_maximum_fusion.13), channel_id=1, source_target_pairs={{4,0},{8,4},{12,8},{16,12},{20,16},{24,20},{28,24},{5,1},{9,5},{13... | collective-permute-start | bytes 49160 | tf_op jit(solution)/shard_map/ppermute | solution.py:29
  216.7 1.1 slice.282
  217.8 1.1 slice.283
  219.0 2.5 %slice.280 = f32[4,511,512]{2,1,0:T(8,128)} slice(f32[4,512,512]{2,1,0:T(8,128)S(1)} %multiply_add_fusion), slice={[0:4], [1:512], [0:512]} | slice | bytes 8372224 | tf_op jit(solution)/shard_map/slice | solution.py:132
  221.5 6.8 %fusion.3 = (f32[4,512,512]{2,1,0:T(8,128)}, f32[4,512,512]{2,1,0:T(8,128)}) fusion(f32[4,512,512]{2,1,0:T(8,128)S(1)} %multiply_add_fusion, f32[4,512,511]{2,1,0:T(8,128)S(1)} %slice.283, f32[4,512,512]{2,1,0:T(8,128)S(1)} %copy-done.1, f32[4,512,511]{2,1,0:T(8,128)S(1)} %slice.282, f32[4,1,512]{2,1,0:T(1,128)S(1)} %get-tuple-element.194, ...), kind=kLoop, calls=%fused_computation.14 | loop fusion | flops 17825792 | bytes 33538048 | tf_op jit(solution)/shard_map/mul | solution.py:136
  (84 shorter events, 11.6 us)
Async XLA Ops:
  7.2 160.5 %all-gather.3.cloned.1.call-start = ((), (), s32[]{:S(2)}) async-start(), calls=%async_computation | async-start | bytes 10485760 | tf_op jit(solution)/shard_map/all_gather | solution.py:115
  15.0 8.8 %copy-start.13 = (u32[32]{0:T(128)S(1)}, u32[32]{0:T(128)}, u32[]{:S(2)}) copy-start(u32[32]{0:T(128)} %constant.82) | copy-start | bytes 388
  15.0 10.0 %copy-start.12 = (f32[4]{0:T(128)S(1)}, f32[4]{0:T(128)}, u32[]{:S(2)}) copy-start(f32[4]{0:T(128)} %param.12) | copy-start | bytes 52
  15.0 23.4 %copy-start.2 = (s32[512,512]{1,0:T(8,128)S(1)}, s32[512,512]{1,0:T(8,128)}, u32[]{:S(2)}) copy-start(s32[512,512]{1,0:T(8,128)} %param.13) | copy-start | bytes 3145732
  15.0 23.4 %copy-start.4 = (s32[512,512]{1,0:T(8,128)S(1)}, s32[512,512]{1,0:T(8,128)}, u32[]{:S(2)}) copy-start(s32[512,512]{1,0:T(8,128)} %param.14) | copy-start | bytes 3145732
  17.3 161.5 %collective-permute-start.2 = (f32[1,512]{1,0:T(1,128)S(1)}, f32[1,512]{1,0:T(1,128)S(1)}, u32[]{:S(2)}, u32[]{:S(2)}) collective-permute-start(f32[1,512]{1,0:T(1,128)S(1)} %get-tuple-element.191), channel_id=1, source_target_pairs={{0,4},{4,8},{8,12},{12,16},{16,20},{20,24},{24,28},{1,5},{5,9},{9,... | collective-permute-start | bytes 6152 | tf_op jit(solution)/shard_map/ppermute | solution.py:18
  19.2 159.6 %collective-permute-start.3 = (f32[1,512]{1,0:T(1,128)S(1)}, f32[1,512]{1,0:T(1,128)S(1)}, u32[]{:S(2)}, u32[]{:S(2)}) collective-permute-start(f32[1,512]{1,0:T(1,128)S(1)} %get-tuple-element.192), channel_id=1, source_target_pairs={{4,0},{8,4},{12,8},{16,12},{20,16},{24,20},{28,24},{5,1},{9,5},{13... | collective-permute-start | bytes 6152 | tf_op jit(solution)/shard_map/ppermute | solution.py:21
  38.4 1.4 copy-start.6
  40.6 1.0 copy-start.7
  41.5 1.4 copy-start.6
  43.7 1.0 copy-start.7
  44.7 1.4 copy-start.6
  46.9 1.0 copy-start.7
  47.8 1.4 copy-start.6
  50.0 1.0 copy-start.7
  172.3 8.2 %collective-permute-start = (f32[3,1,512]{2,1,0:T(1,128)S(1)}, f32[3,1,512]{2,1,0:T(1,128)S(1)}, u32[]{:S(2)}, u32[]{:S(2)}) collective-permute-start(f32[3,1,512]{2,1,0:T(1,128)S(1)} %get-tuple-element.185), channel_id=1, source_target_pairs={{0,4},{4,8},{8,12},{12,16},{16,20},{20,24},{24,28},{1,5},{5,9},{9,... | collective-permute-start | bytes 18440 | tf_op jit(solution)/shard_map/ppermute | solution.py:18
  174.2 6.2 %collective-permute-start.1 = (f32[3,1,512]{2,1,0:T(1,128)S(1)}, f32[3,1,512]{2,1,0:T(1,128)S(1)}, u32[]{:S(2)}, u32[]{:S(2)}) collective-permute-start(f32[3,1,512]{2,1,0:T(1,128)S(1)} %get-tuple-element.186), channel_id=1, source_target_pairs={{4,0},{8,4},{12,8},{16,12},{20,16},{24,20},{28,24},{5,1},{9,5},{13... | collective-permute-start | bytes 18440 | tf_op jit(solution)/shard_map/ppermute | solution.py:21
  180.9 1.2 copy-start.9
  180.9 1.5 copy-start.10
  180.9 1.8 copy-start.11
  182.8 13.0 %copy-start.8 = (f32[512,512]{1,0:T(8,128)S(1)}, f32[512,512]{1,0:T(8,128)}, u32[]{:S(2)}) copy-start(f32[512,512]{1,0:T(8,128)} %get-tuple-element.129) | copy-start | bytes 3145732
  189.2 7.2 %collective-permute-start.4 = (f32[1,512]{1,0:T(1,128)S(1)}, f32[1,512]{1,0:T(1,128)S(1)}, u32[]{:S(2)}, u32[]{:S(2)}) collective-permute-start(f32[1,512]{1,0:T(1,128)S(1)} %get-tuple-element.189), channel_id=1, source_target_pairs={{0,4},{4,8},{8,12},{12,16},{16,20},{20,24},{24,28},{1,5},{5,9},{9,... | collective-permute-start | bytes 6152 | tf_op jit(solution)/shard_map/ppermute | solution.py:18
  191.4 5.6 %collective-permute-start.5 = (f32[1,512]{1,0:T(1,128)S(1)}, f32[1,512]{1,0:T(1,128)S(1)}, u32[]{:S(2)}, u32[]{:S(2)}) collective-permute-start(f32[1,512]{1,0:T(1,128)S(1)} %get-tuple-element.190), channel_id=1, source_target_pairs={{4,0},{8,4},{12,8},{16,12},{20,16},{24,20},{28,24},{5,1},{9,5},{13... | collective-permute-start | bytes 6152 | tf_op jit(solution)/shard_map/ppermute | solution.py:21
  197.4 8.4 %copy-start.1 = (f32[4,512,512]{2,1,0:T(8,128)S(1)}, f32[4,512,512]{2,1,0:T(8,128)}, u32[]{:S(2)}) copy-start(f32[4,512,512]{2,1,0:T(8,128)} %get-tuple-element.176) | copy-start | bytes 12582916
  199.2 6.7 %collective-permute-start.6 = (f32[1,512]{1,0:T(1,128)S(1)}, f32[1,512]{1,0:T(1,128)S(1)}, u32[]{:S(2)}, u32[]{:S(2)}) collective-permute-start(f32[1,512]{1,0:T(1,128)S(1)} %get-tuple-element.187), channel_id=1, source_target_pairs={{0,4},{4,8},{8,12},{12,16},{16,20},{20,24},{24,28},{1,5},{5,9},{9,... | collective-permute-start | bytes 6152 | tf_op jit(solution)/shard_map/ppermute | solution.py:18
  201.2 5.8 %collective-permute-start.7 = (f32[1,512]{1,0:T(1,128)S(1)}, f32[1,512]{1,0:T(1,128)S(1)}, u32[]{:S(2)}, u32[]{:S(2)}) collective-permute-start(f32[1,512]{1,0:T(1,128)S(1)} %get-tuple-element.188), channel_id=1, source_target_pairs={{4,0},{8,4},{12,8},{16,12},{20,16},{24,20},{28,24},{5,1},{9,5},{13... | collective-permute-start | bytes 6152 | tf_op jit(solution)/shard_map/ppermute | solution.py:21
  207.5 1.8 copy-start.3
  207.5 1.8 copy-start.5
  211.4 10.0 %copy-start = (f32[4,512,512]{2,1,0:T(8,128)}, f32[4,512,512]{2,1,0:T(8,128)S(1)}, u32[]{:S(2)}) copy-start(f32[4,512,512]{2,1,0:T(8,128)S(1)} %multiply_add_fusion) | copy-start | bytes 12582916
  211.5 10.0 %collective-permute-start.8 = (f32[2,4,512]{2,0,1:T(2,128)S(1)}, f32[2,4,512]{2,0,1:T(2,128)S(1)}, u32[]{:S(2)}, u32[]{:S(2)}) collective-permute-start(f32[2,4,512]{2,0,1:T(2,128)S(1)} %pad_maximum_fusion.13), channel_id=1, source_target_pairs={{4,0},{8,4},{12,8},{16,12},{20,16},{24,20},{28,24},{5,1},{9,5},{13... | collective-permute-start | bytes 49160 | tf_op jit(solution)/shard_map/ppermute | solution.py:29
Sparse Core Ops, SparseCore 0:
  16.6 150.9 all-gather.2
